TPU v7x, 32 devices: a whole 2x2x4 slice. The times are simulated.
32 devices in a mesh: dp: 8 (over y, x, core), mp: 4 (over z).
Axes of the slice: x: 2, y: 2, z: 4, core: 2. Of those that a mesh axis runs over, the one named last changes fastest.
Arguments:
- hidden_in: bfloat16 [2, 8192, 2048], P(None, ('dp', 'mp')), may hold values from -6 to 6
- counts: int32 [2, 8], P(None, 'dp'), may hold values from 20 to 50, as said below
- summary: float32 [50, 2048], replicated, may hold values from -6 to 6
- query_weight: bfloat16 [2048, 2048], P('dp', 'mp'), may hold values from -0.125 to 0.125
- query_bias: bfloat16 [2048], P('mp'), may hold values from -1.75 to 1.75
- key_weight: bfloat16 [2048, 2048], P('dp', 'mp'), may hold values from -0.125 to 0.125
- value_weight: bfloat16 [2048, 2048], P('dp', 'mp'), may hold values from -0.125 to 0.125
- value_bias: bfloat16 [2048], P('mp'), may hold values from -1.75 to 1.75
- out_weight: bfloat16 [2048, 2048], P('mp', 'dp'), may hold values from -2 to 2
- out_bias: bfloat16 [2048], replicated, may hold values from -1.25 to 1.25
- up_weight: bfloat16 [2048, 8192], P('dp', 'mp'), may hold values from -0.125 to 0.125
- up_bias: bfloat16 [8192], P('mp'), may hold values from -1.75 to 1.75
- down_weight: bfloat16 [8192, 2048], P('mp', 'dp'), may hold values from -0.0625 to 0.0625
- down_bias: bfloat16 [2048], replicated, may hold values from -1.25 to 1.25
- attn_gain: float32 [2048], replicated, may hold values from 0.5 to 1.5
- attn_shift: float32 [2048], replicated, may hold values from -0.625 to 0.625
- mlp_gain: float32 [2048], replicated, may hold values from 0.5 to 1.5
- mlp_shift: float32 [2048], replicated, may hold values from -0.625 to 0.625
- cotangent: bfloat16 [2, 8192, 2048], P(None, ('dp', 'mp')), may hold values from -6 to 6
Outputs:
- layer_out: bfloat16 [2, 8192, 2048], P(None, ('dp', 'mp'))
- grad_input: float32 [2, 8192, 2048], P(None, ('dp', 'mp'))
- grad_summary: float32 [50, 2048], replicated
- grad_query_weight: float32 [2048, 2048], P('dp', 'mp')
- grad_query_bias: float32 [2048], P('mp')
- grad_key_weight: float32 [2048, 2048], P('dp', 'mp')
- grad_value_weight: float32 [2048, 2048], P('dp', 'mp')
- grad_value_bias: float32 [2048], P('mp')
- grad_out_weight: float32 [2048, 2048], P('mp', 'dp')
- grad_out_bias: float32 [2048], replicated
- grad_up_weight: float32 [2048, 8192], P('dp', 'mp')
- grad_up_bias: float32 [8192], P('mp')
- grad_down_weight: float32 [8192, 2048], P('mp', 'dp')
- grad_down_bias: float32 [2048], replicated
- grad_attn_gain: float32 [2048], replicated
- grad_attn_shift: float32 [2048], replicated
- grad_mlp_gain: float32 [2048], replicated
- grad_mlp_shift: float32 [2048], replicated
Inputs may be any that keep to these rules, and one draw needn't show every extreme that they name: `counts`: an item's count c marks the first c of its 50 prefix slots and the first c of its 50 appended slots as used.
All inputs are finite; a program needn't handle non-finite values.
Results may differ from a plain program's by a relative error of at most 0.02.
Values may be sent and summed in bfloat16 or wider, within the bound.
No kernel may reach another device: no remote copies, remote signals or barrier semaphores. Data moves between devices by JAX's collectives and lax.ppermute only.
A program may use at most 256 MiB of HBM per device.

v0:
```python
import math
import jax
import jax.numpy as jnp
from jax import lax
from jax.sharding import PartitionSpec as P

D = 2048
HD = 64
SUMM = 50
precise = lax.Precision.HIGHEST
gelu_coef = math.sqrt(2.0 / math.pi)


def gelu_slope(values_in):
    inner = gelu_coef * (values_in + 0.044715 * values_in * values_in * values_in)
    tangent = jnp.tanh(inner)
    return 0.5 * (1.0 + tangent) + 0.5 * values_in * (1.0 - tangent * tangent) * gelu_coef * (
        1.0 + 3.0 * 0.044715 * values_in * values_in
    )


def layer_norm(values_in, gain_vec, shift_vec):
    centred = values_in - jnp.mean(values_in, axis=-1, keepdims=True)
    spread = jnp.mean(centred * centred, axis=-1, keepdims=True)
    scaled = lax.rsqrt(spread + 1e-05)
    unit_rows = centred * scaled
    return (unit_rows * gain_vec + shift_vec, unit_rows, scaled)


def norm_back(grad_out, unit_rows, scaled, gain_vec):
    weighted = grad_out * gain_vec
    return scaled * (
        weighted
        - jnp.mean(weighted, axis=-1, keepdims=True)
        - unit_rows * jnp.mean(weighted * unit_rows, axis=-1, keepdims=True)
    )


def dense(left_side, right_side):
    return jnp.dot(left_side, right_side, preferred_element_type=jnp.float32)


def times_t(left_side, right_side):
    return lax.dot_general(
        left_side, right_side, (((1,), (1,)), ((), ())), preferred_element_type=jnp.float32
    )


def inner_rows(left_side, right_side):
    return lax.dot_general(
        left_side, right_side, (((0,), (0,)), ((), ())), preferred_element_type=jnp.float32
    )


def live_keys(seq_len, item_count):
    positions = jnp.arange(seq_len, dtype=jnp.int32)
    slot_ids = positions - (seq_len - SUMM)
    return (
        (positions >= SUMM) & (slot_ids < 0)
        | (positions < item_count)
        | (slot_ids >= 0) & (slot_ids < item_count)
    )


def block_mask(row_begin, block_rows, key_live):
    rows_here = row_begin + jnp.arange(block_rows, dtype=jnp.int32)
    columns = jnp.arange(key_live.shape[0], dtype=jnp.int32)
    return (columns[None, :] <= rows_here[:, None]) & key_live[None, :]


def shards(
    hidden_in,
    counts,
    summary,
    query_weight,
    query_bias,
    key_weight,
    value_weight,
    value_bias,
    out_weight,
    out_bias,
    up_weight,
    up_bias,
    down_weight,
    down_bias,
    attn_gain,
    attn_shift,
    mlp_gain,
    mlp_shift,
    cotangent,
):
    micro_total = hidden_in.shape[0]
    local_rows = hidden_in.shape[1]
    seq_len = local_rows * lax.axis_size("mp")
    row_offset = lax.axis_index("mp") * local_rows
    head_cols = query_weight.shape[1]
    ff_cols = up_weight.shape[1]
    local_heads = head_cols // HD
    block_rows = 512
    block_count = seq_len // block_rows
    qk_scale = HD ** (-0.5)
    bias_query = query_bias.astype(jnp.float32)
    bias_value = value_bias.astype(jnp.float32)
    bias_up = up_bias.astype(jnp.float32)
    bias_out = out_bias.astype(jnp.float32)
    bias_down = down_bias.astype(jnp.float32)
    positions = row_offset + jnp.arange(local_rows, dtype=jnp.int32)
    picker = (
        (positions - (seq_len - SUMM))[:, None] == jnp.arange(SUMM, dtype=jnp.int32)[None, :]
    ).astype(jnp.float32)
    summary_rows = jnp.dot(picker, summary, precision=precise)
    full_shapes = (
        (D, head_cols),
        (D, head_cols),
        (D, head_cols),
        (head_cols, D),
        (D, ff_cols),
        (ff_cols, D),
    )
    full_sums = tuple((jnp.zeros(shape_pair, jnp.float32) for shape_pair in full_shapes))
    head_sums = (
        jnp.zeros((head_cols,), jnp.float32),
        jnp.zeros((head_cols,), jnp.float32),
        jnp.zeros((ff_cols,), jnp.float32),
    )
    zero_width = jnp.zeros((D,), jnp.float32)
    row_sums = (
        zero_width,
        zero_width,
        zero_width,
        zero_width,
        zero_width,
        zero_width,
        jnp.zeros((SUMM, D), jnp.float32),
    )
    outputs = []
    input_grads = []
    for micro_step in range(micro_total):
        gathered = (
            lax.all_gather(query_weight, "dp", axis=0, tiled=True),
            lax.all_gather(key_weight, "dp", axis=0, tiled=True),
            lax.all_gather(value_weight, "dp", axis=0, tiled=True),
            lax.all_gather(out_weight, "dp", axis=1, tiled=True),
            lax.all_gather(up_weight, "dp", axis=0, tiled=True),
            lax.all_gather(down_weight, "dp", axis=1, tiled=True),
        )
        query_full, key_full, value_full, out_full, up_full, down_full = gathered
        key_live = live_keys(seq_len, counts[micro_step, 0])
        joined = hidden_in[micro_step].astype(jnp.float32) + summary_rows
        normed, unit_one, scale_one = layer_norm(joined, attn_gain, attn_shift)
        shard_rows = lax.all_gather(normed.astype(jnp.bfloat16), "mp", axis=0, tiled=True)
        query_part = ((dense(shard_rows, query_full) + bias_query) * qk_scale).astype(jnp.bfloat16)
        key_part = dense(shard_rows, key_full).astype(jnp.bfloat16)
        value_part = (dense(shard_rows, value_full) + bias_value).astype(jnp.bfloat16)
        projected = jnp.concatenate((shard_rows, query_part, key_part, value_part), axis=1)
        normed_full = projected[:, :D]
        query_rows = projected[:, D : D + head_cols].reshape(seq_len, local_heads, HD)
        key_rows = projected[:, D + head_cols : D + 2 * head_cols].reshape(seq_len, local_heads, HD)
        value_rows = projected[:, D + 2 * head_cols :].reshape(seq_len, local_heads, HD)

        def forward_block(block_index):
            row_begin = block_index * block_rows
            query_block = lax.dynamic_slice_in_dim(query_rows, row_begin, block_rows, 0)
            scores = jnp.einsum(
                "qhd,khd->hqk", query_block, key_rows, preferred_element_type=jnp.float32
            )
            scores = jnp.where(block_mask(row_begin, block_rows, key_live)[None], scores, -1e30)
            row_top = jnp.max(scores, axis=-1, keepdims=True)
            exp_scores = jnp.exp(scores - row_top)
            exp_total = jnp.sum(exp_scores, axis=-1, keepdims=True)
            weights_low = (exp_scores / exp_total).astype(jnp.bfloat16)
            block_out = jnp.einsum(
                "hqk,khd->qhd", weights_low, value_rows, preferred_element_type=jnp.float32
            )
            return (
                block_out.astype(jnp.bfloat16).reshape(block_rows, head_cols),
                (row_top + jnp.log(exp_total))[..., 0],
            )

        attn_blocks, log_totals = lax.map(forward_block, jnp.arange(block_count, dtype=jnp.int32))
        attended = attn_blocks.reshape(seq_len, head_cols)
        mixed_rows = (
            joined
            + lax.psum_scatter(
                dense(attended, out_full).astype(jnp.bfloat16),
                "mp",
                scatter_dimension=0,
                tiled=True,
            ).astype(jnp.float32)
            + bias_out
        )
        normed_two, unit_two, scale_two = layer_norm(mixed_rows, mlp_gain, mlp_shift)
        expand_shard_rows = lax.all_gather(
            normed_two.astype(jnp.bfloat16), "mp", axis=0, tiled=True
        )
        up_value = dense(expand_shard_rows, up_full) + bias_up
        expanded = jnp.concatenate(
            (expand_shard_rows, jax.nn.gelu(up_value, approximate=True).astype(jnp.bfloat16)),
            axis=1,
        )
        normed_two_full = expanded[:, :D]
        active = expanded[:, D:]
        layer_rows = (
            mixed_rows
            + lax.psum_scatter(
                dense(active, down_full).astype(jnp.bfloat16), "mp", scatter_dimension=0, tiled=True
            ).astype(jnp.float32)
            + bias_down
        )
        outputs.append(layer_rows.astype(jnp.bfloat16))
        grad_rows = cotangent[micro_step]
        grad_layer = grad_rows.astype(jnp.float32)
        mlp_shard_rows = lax.all_gather(grad_rows, "mp", axis=0, tiled=True)
        mlp_up_value = dense(normed_two_full, up_full) + bias_up
        grad_active = times_t(mlp_shard_rows, down_full)
        mlp_grad_up = (grad_active * gelu_slope(mlp_up_value)).astype(jnp.bfloat16)
        spread_grads = jnp.concatenate((mlp_shard_rows, mlp_grad_up), axis=1)
        grad_full = spread_grads[:, :D]
        grad_up = spread_grads[:, D:]
        micro_down = inner_rows(active, grad_full)
        micro_up = inner_rows(normed_two_full, grad_up)
        up_bias_grad = jnp.sum(grad_up.astype(jnp.float32), axis=0)
        grad_normed_two = lax.psum_scatter(
            times_t(grad_up, up_full).astype(jnp.bfloat16), "mp", scatter_dimension=0, tiled=True
        ).astype(jnp.float32)
        grad_mixed = grad_layer + norm_back(grad_normed_two, unit_two, scale_two, mlp_gain)
        attn_shard_rows = lax.all_gather(grad_mixed.astype(jnp.bfloat16), "mp", axis=0, tiled=True)
        spread_attn = jnp.concatenate(
            (attn_shard_rows, times_t(attn_shard_rows, out_full).astype(jnp.bfloat16)), axis=1
        )
        grad_mixed_full = spread_attn[:, :D]
        grad_attended = spread_attn[:, D:].reshape(seq_len, local_heads, HD)
        micro_out = inner_rows(attended, grad_mixed_full)

        def backward_block(sums_pair, block_index):
            key_sum, value_sum = sums_pair
            row_begin = block_index * block_rows
            query_block = lax.dynamic_slice_in_dim(query_rows, row_begin, block_rows, 0)
            grad_block = lax.dynamic_slice_in_dim(grad_attended, row_begin, block_rows, 0)
            scores = jnp.einsum(
                "qhd,khd->hqk", query_block, key_rows, preferred_element_type=jnp.float32
            )
            scores = jnp.where(block_mask(row_begin, block_rows, key_live)[None], scores, -1e30)
            weights_full = jnp.exp(scores - log_totals[block_index][..., None])
            grad_weights = jnp.einsum(
                "qhd,khd->hqk", grad_block, value_rows, preferred_element_type=jnp.float32
            )
            centre = jnp.sum(weights_full * grad_weights, axis=-1, keepdims=True)
            grad_scores = (weights_full * (grad_weights - centre)).astype(jnp.bfloat16)
            grad_query_block = jnp.einsum(
                "hqk,khd->qhd", grad_scores, key_rows, preferred_element_type=jnp.float32
            )
            key_sum = key_sum + jnp.einsum(
                "hqk,qhd->khd", grad_scores, query_block, preferred_element_type=jnp.float32
            )
            value_sum = value_sum + jnp.einsum(
                "hqk,qhd->khd",
                weights_full.astype(jnp.bfloat16),
                grad_block,
                preferred_element_type=jnp.float32,
            )
            return (
                (key_sum, value_sum),
                grad_query_block.astype(jnp.bfloat16).reshape(block_rows, head_cols),
            )

        zero_heads = jnp.zeros((seq_len, local_heads, HD), jnp.float32)
        (key_sum, value_sum), query_blocks = lax.scan(
            backward_block, (zero_heads, zero_heads), jnp.arange(block_count, dtype=jnp.int32)
        )
        grad_query = query_blocks.reshape(seq_len, head_cols)
        grad_key = key_sum.astype(jnp.bfloat16).reshape(seq_len, head_cols)
        grad_value = value_sum.astype(jnp.bfloat16).reshape(seq_len, head_cols)
        micro_query = inner_rows(normed_full, grad_query) * qk_scale
        micro_key = inner_rows(normed_full, grad_key)
        micro_value = inner_rows(normed_full, grad_value)
        query_bias_grad = jnp.sum(grad_query.astype(jnp.float32), axis=0) * qk_scale
        value_bias_grad = jnp.sum(grad_value.astype(jnp.float32), axis=0)
        grad_normed = lax.psum_scatter(
            (
                times_t(grad_query, query_full) * qk_scale
                + times_t(grad_key, key_full)
                + times_t(grad_value, value_full)
            ).astype(jnp.bfloat16),
            "mp",
            scatter_dimension=0,
            tiled=True,
        ).astype(jnp.float32)
        grad_joined = grad_mixed + norm_back(grad_normed, unit_one, scale_one, attn_gain)
        input_grads.append(grad_joined)
        micro_grads = (micro_query, micro_key, micro_value, micro_out, micro_up, micro_down)
        full_sums = tuple(map(jnp.add, full_sums, micro_grads))
        head_sums = (
            head_sums[0] + query_bias_grad,
            head_sums[1] + value_bias_grad,
            head_sums[2] + up_bias_grad,
        )
        row_sums = (
            row_sums[0] + jnp.sum(grad_mixed, axis=0),
            row_sums[1] + jnp.sum(grad_layer, axis=0),
            row_sums[2] + jnp.sum(grad_normed * unit_one, axis=0),
            row_sums[3] + jnp.sum(grad_normed, axis=0),
            row_sums[4] + jnp.sum(grad_normed_two * unit_two, axis=0),
            row_sums[5] + jnp.sum(grad_normed_two, axis=0),
            row_sums[6] + jnp.dot(picker.T, grad_joined, precision=precise),
        )
    weight_total = (
        lax.psum_scatter(
            full_sums[0].astype(jnp.bfloat16), "dp", scatter_dimension=0, tiled=True
        ).astype(jnp.float32),
        lax.psum_scatter(
            full_sums[1].astype(jnp.bfloat16), "dp", scatter_dimension=0, tiled=True
        ).astype(jnp.float32),
        lax.psum_scatter(
            full_sums[2].astype(jnp.bfloat16), "dp", scatter_dimension=0, tiled=True
        ).astype(jnp.float32),
        lax.psum_scatter(
            full_sums[3].astype(jnp.bfloat16), "dp", scatter_dimension=1, tiled=True
        ).astype(jnp.float32),
        lax.psum_scatter(
            full_sums[4].astype(jnp.bfloat16), "dp", scatter_dimension=0, tiled=True
        ).astype(jnp.float32),
        lax.psum_scatter(
            full_sums[5].astype(jnp.bfloat16), "dp", scatter_dimension=1, tiled=True
        ).astype(jnp.float32),
    )
    head_total = lax.psum((head_sums[0], head_sums[1], head_sums[2]), "dp")
    row_total = lax.psum(
        (row_sums[0], row_sums[1], row_sums[2], row_sums[3], row_sums[4], row_sums[5], row_sums[6]),
        ("dp", "mp"),
    )
    return (
        jnp.stack(outputs),
        jnp.stack(input_grads),
        row_total[6],
        weight_total[0],
        head_total[0],
        weight_total[1],
        weight_total[2],
        head_total[1],
        weight_total[3],
        row_total[0],
        weight_total[4],
        head_total[2],
        weight_total[5],
        row_total[1],
        row_total[2],
        row_total[3],
        row_total[4],
        row_total[5],
    )


def solution(mesh):
    in_specs = (
        P(None, ("dp", "mp"), None),
        P(None, "dp"),
        P(),
        P("dp", "mp"),
        P("mp"),
        P("dp", "mp"),
        P("dp", "mp"),
        P("mp"),
        P("mp", "dp"),
        P(),
        P("dp", "mp"),
        P("mp"),
        P("mp", "dp"),
        P(),
        P(),
        P(),
        P(),
        P(),
        P(None, ("dp", "mp"), None),
    )
    out_specs = (
        P(None, ("dp", "mp"), None),
        P(None, ("dp", "mp"), None),
        P(),
        P("dp", "mp"),
        P("mp"),
        P("dp", "mp"),
        P("dp", "mp"),
        P("mp"),
        P("mp", "dp"),
        P(),
        P("dp", "mp"),
        P("mp"),
        P("mp", "dp"),
        P(),
        P(),
        P(),
        P(),
        P(),
    )
    return jax.shard_map(shards, mesh=mesh, in_specs=in_specs, out_specs=out_specs, check_vma=False)
```

profile of v0, /device:TPU:1, one launch (start us, length us, event | category | flops | bytes accessed | tf_op | source)
XLA Modules:
  0.0 2053.1 jit_solution(16066606750939423374)
XLA Ops:
  17.3 23.1 %all-gather.21.cloned.1.call-done = bf16[2048,512]{1,0:T(8,128)(2,1)} async-done(((bf16[256,512]{1,0:T(8,128)(2,1)}), bf16[2048,512]{1,0:T(8,128)(2,1)}) %all-gather.21.cloned.1.call-update) | async-done | bytes 2097168 | tf_op jit(solution)/shard_map/all_gather | solution.py:141
  40.4 82.5 %all-gather.17.cloned.1.call-done = bf16[1024,2048]{1,0:T(8,128)(2,1)} async-done(((bf16[256,2048]{1,0:T(8,128)(2,1)}), bf16[1024,2048]{1,0:T(8,128)(2,1)}) %all-gather.17.cloned.1.call-update) | async-done | bytes 4194320 | tf_op jit(solution)/shard_map/all_gather | solution.py:151
  128.1 23.5 %all-gather.19.cloned.1.call-done = bf16[2048,512]{1,0:T(8,128)(2,1)} async-done(((bf16[256,512]{1,0:T(8,128)(2,1)}), bf16[2048,512]{1,0:T(8,128)(2,1)}) %all-gather.19.cloned.1.call-update) | async-done | bytes 2097168 | tf_op jit(solution)/shard_map/all_gather | solution.py:140
  156.9 24.4 %all-gather.23.cloned.1.call-done = bf16[2048,512]{1,0:T(8,128)(2,1)} async-done(((bf16[256,512]{1,0:T(8,128)(2,1)}), bf16[2048,512]{1,0:T(8,128)(2,1)}) %all-gather.23.cloned.1.call-update) | async-done | bytes 2097168 | tf_op jit(solution)/shard_map/all_gather | solution.py:142
  188.6 33.1 %while.56 = (s32[]{:T(128)}, bf16[2,512,512]{2,1,0:T(8,128)(2,1)}, f32[2,8,512]{2,1,0:T(8,128)S(1)}, s32[2]{0:T(128)S(1)}, bf16[1024,8,64]{0,2,1:T(8,128)(2,1)S(...) while((s32[]{:T(128)}, bf16[2,512,512]{2,1,0:T(8,128)(2,1)}, ...), condition=%wide.region_5.6_spmd.clone, body=%wide.region_2.5_spmd.clone.sunk | while | flops 1112807936 | bytes 62003432 | solution.py:180
  229.3 64.5 %all-gather.33.cloned.1.call-done = bf16[1024,2048]{1,0:T(8,128)(2,1)} async-done(((bf16[256,2048]{1,0:T(8,128)(2,1)}), bf16[1024,2048]{1,0:T(8,128)(2,1)}) %all-gather.33.cloned.1.call-update) | async-done | bytes 4194320 | tf_op jit(solution)/shard_map/all_gather | solution.py:151
  307.8 33.3 %while.57 = (s32[]{:T(128)}, bf16[2,512,512]{2,1,0:T(8,128)(2,1)}, f32[2,8,512]{2,1,0:T(8,128)S(1)}, s32[2]{0:T(128)S(1)}, bf16[1024,8,64]{0,2,1:T(8,128)(2,1)S(...) while((s32[]{:T(128)}, bf16[2,512,512]{2,1,0:T(8,128)(2,1)}, ...), condition=%wide.region_15.16_spmd.clone, body=%wide.region_12.15_spmd.clone.sunk | while | flops 1112807936 | bytes 62003432 | solution.py:180
  349.1 22.8 %reduce-scatter.15.cloned.1.call-done = bf16[256,2048]{1,0:T(8,128)(2,1)} async-done(((bf16[1024,2048]{1,0:T(8,128)(2,1)}), bf16[256,2048]{1,0:T(8,128)(2,1)}) %reduce-scatter.15.cloned.1.call-update) | async-done | bytes 1048592 | tf_op jit(solution)/shard_map/reduce_scatter | solution.py:184
  371.9 79.7 %reduce-scatter.19.cloned.1.call-done = bf16[256,2048]{1,0:T(8,128)(2,1)} async-done(((bf16[1024,2048]{1,0:T(8,128)(2,1)}), bf16[256,2048]{1,0:T(8,128)(2,1)}) %reduce-scatter.19.cloned.1.call-update) | async-done | bytes 1048592 | tf_op jit(solution)/shard_map/reduce_scatter | solution.py:184
  461.7 47.2 %all-gather.29.cloned.1.call-done = bf16[2048,2048]{1,0:T(8,128)(2,1)} async-done(((bf16[256,2048]{1,0:T(8,128)(2,1)}), bf16[2048,2048]{1,0:T(8,128)(2,1)}) %all-gather.29.cloned.1.call-update) | async-done | bytes 8388624 | tf_op jit(solution)/shard_map/all_gather | solution.py:144
  508.8 82.4 %all-gather.27.cloned.1.call-done = bf16[1024,2048]{1,0:T(8,128)(2,1)} async-done(((bf16[256,2048]{1,0:T(8,128)(2,1)}), bf16[1024,2048]{1,0:T(8,128)(2,1)}) %all-gather.27.cloned.1.call-update) | async-done | bytes 4194320 | tf_op jit(solution)/shard_map/all_gather | solution.py:193
  605.9 66.8 %all-gather.41.cloned.1.call-done = bf16[1,1024,2048]{2,1,0:T(8,128)(2,1)} async-done(((bf16[1,256,2048]{2,1,0:T(8,128)(2,1)}), bf16[1,1024,2048]{2,1,0:T(8,128)(2,1)}) %all-gather.41.cloned.1.call-update) | async-done | bytes 4194320 | tf_op jit(solution)/shard_map/all_gather | solution.py:213
  672.7 56.7 %all-gather.31.cloned.1.call-done = bf16[2048,2048]{1,0:T(8,128)(2,1)} async-done(((bf16[2048,256]{1,0:T(8,128)(2,1)}), bf16[2048,2048]{1,0:T(8,128)(2,1)}) %all-gather.31.cloned.1.call-update) | async-done | bytes 8388624 | tf_op jit(solution)/shard_map/all_gather | solution.py:145
  729.3 18.8 convert_reduce_fusion.1
  763.2 48.0 %all-gather.35.cloned.1.call-done = bf16[1024,2048]{1,0:T(8,128)(2,1)} async-done(((bf16[256,2048]{1,0:T(8,128)(2,1)}), bf16[1024,2048]{1,0:T(8,128)(2,1)}) %all-gather.35.cloned.1.call-update) | async-done | bytes 4194320 | tf_op jit(solution)/shard_map/all_gather | solution.py:193
  825.8 66.2 %all-gather.43.cloned.1.call-done = bf16[1,1024,2048]{2,1,0:T(8,128)(2,1)} async-done(((bf16[1,256,2048]{2,1,0:T(8,128)(2,1)}), bf16[1,1024,2048]{2,1,0:T(8,128)(2,1)}) %all-gather.43.cloned.1.call-update) | async-done | bytes 4194320 | tf_op jit(solution)/shard_map/all_gather | solution.py:213
  892.0 18.8 convert_reduce_fusion
  942.5 16.2 convolution_convert_fusion.6
  970.1 79.5 %reduce-scatter.27.cloned.1.call-done = bf16[256,2048]{1,0:T(8,128)(2,1)} async-done(((bf16[1024,2048]{1,0:T(8,128)(2,1)}), bf16[256,2048]{1,0:T(8,128)(2,1)}) %reduce-scatter.27.cloned.1.call-update) | async-done | bytes 1048592 | tf_op jit(solution)/shard_map/reduce_scatter | solution.py:223
  1053.8 75.2 %reduce-scatter.21.cloned.1.call-done = bf16[256,2048]{1,0:T(8,128)(2,1)} async-done(((bf16[1024,2048]{1,0:T(8,128)(2,1)}), bf16[256,2048]{1,0:T(8,128)(2,1)}) %reduce-scatter.21.cloned.1.call-update) | async-done | bytes 1048592 | tf_op jit(solution)/shard_map/reduce_scatter | solution.py:205
  1129.1 79.5 %reduce-scatter.17.cloned.1.call-done = bf16[256,2048]{1,0:T(8,128)(2,1)} async-done(((bf16[1024,2048]{1,0:T(8,128)(2,1)}), bf16[256,2048]{1,0:T(8,128)(2,1)}) %reduce-scatter.17.cloned.1.call-update) | async-done | bytes 1048592 | tf_op jit(solution)/shard_map/reduce_scatter | solution.py:205
  1249.2 17.9 fusion.124
  1267.1 21.3 %add_convert_fusion = bf16[2048,2048]{1,0:T(8,128)(2,1)} fusion(f32[2048,2048]{1,0:T(8,128)} %fusion.124, bf16[1,1024,2048]{2,1,0:T(8,128)(2,1)S(1)} %copy-done.106, f32[1024,2048]{1,0:T(8,128)} %fusion.181, f32[2048]{0:T(1024)S(1)} %convert_element_type.266), kind=kOutput, calls=%fused_computation.128 | convolution fusion | flops 8619294720 | bytes 37756928 | tf_op jit(solution)/shard_map/dot_general | solution.py:50
  1306.4 122.1 %while.59 = (s32[]{:T(128)}, f32[1024,8,64]{0,2,1:T(8,128)}, f32[1024,8,64]{0,2,1:T(8,128)}, bf16[2,512,512]{1,2,0:T(8,128)(2,1)}, s32[2]{0:T(128)S(1)}, /*index...) while((s32[]{:T(128)}, f32[1024,8,64]{0,2,1:T(8,128)}, ...), condition=%wide.region_34.35_spmd.clone, body=%wide.region_32.34_spmd.clone.sunk | while | flops 2738100736 | bytes 252303984 | solution.py:268
  1438.5 122.9 %while.58 = (s32[]{:T(128)}, f32[1024,8,64]{0,2,1:T(8,128)}, f32[1024,8,64]{0,2,1:T(8,128)}, bf16[2,512,512]{1,2,0:T(8,128)(2,1)}, s32[2]{0:T(128)S(1)}, /*index...) while((s32[]{:T(128)}, f32[1024,8,64]{0,2,1:T(8,128)}, ...), condition=%wide.region_25.26_spmd.clone, body=%wide.region_23.25_spmd.clone.sunk | while | flops 2738100736 | bytes 252303984 | solution.py:268
  1641.3 22.2 %all-reduce.1 = (f32[512]{0:T(512)}, f32[512]{0:T(512)}, f32[2048]{0:T(1024)}) all-reduce(f32[512]{0:T(512)S(1)} %add_multiply_fusion, f32[512]{0:T(512)S(1)} %add.506, f32[2048]{0:T(1024)S(1)} %add.510), channel_id=1, replica_groups=mesh['dp'=8,'mp'=4] {'dp'}, use_global_device_ids=true, to_apply=%region_42.43 | all-reduce | flops 3072 | bytes 24576 | tf_op jit(solution)/shard_map/psum | solution.py:327
  1667.2 35.3 %reduce-scatter.35.cloned.1.call-done = bf16[256,512]{1,0:T(8,128)(2,1)} async-done(((bf16[2048,512]{1,0:T(8,128)(2,1)}), bf16[256,512]{1,0:T(8,128)(2,1)}) %reduce-scatter.35.cloned.1.call-update) | async-done | bytes 262160 | tf_op jit(solution)/shard_map/reduce_scatter | solution.py:314
  1704.3 42.9 %reduce-scatter.37.cloned.1.call-done = bf16[512,256]{1,0:T(8,128)(2,1)} async-done(((bf16[512,2048]{1,0:T(8,128)(2,1)}), bf16[512,256]{1,0:T(8,128)(2,1)}) %reduce-scatter.37.cloned.1.call-update) | async-done | bytes 262160 | tf_op jit(solution)/shard_map/reduce_scatter | solution.py:317
  1749.0 77.2 %reduce-scatter.25.cloned.1.call-done = bf16[256,2048]{1,0:T(8,128)(2,1)} async-done(((bf16[1024,2048]{1,0:T(8,128)(2,1)}), bf16[256,2048]{1,0:T(8,128)(2,1)}) %reduce-scatter.25.cloned.1.call-update) | async-done | bytes 1048592 | tf_op jit(solution)/shard_map/reduce_scatter | solution.py:279
  1828.4 78.0 %reduce-scatter.29.cloned.1.call-done = bf16[256,2048]{1,0:T(8,128)(2,1)} async-done(((bf16[1024,2048]{1,0:T(8,128)(2,1)}), bf16[256,2048]{1,0:T(8,128)(2,1)}) %reduce-scatter.29.cloned.1.call-update) | async-done | bytes 1048592 | tf_op jit(solution)/shard_map/reduce_scatter | solution.py:279
  1916.6 41.8 %all-reduce = (f32[2048]{0:T(1024)}, f32[2048]{0:T(1024)}, f32[2048]{0:T(1024)}, f32[2048]{0:T(1024)}, f32[2048]{0:T(1024)}, /*index=5*/f32[2048]{0:T(1024)}) all-reduce(f32[2048]{0:T(1024)S(1)} %add.508, f32[2048]{0:T(1024)S(1)} %add.512, f32[2048]{0:T(1024)S(1)} %add.513, ...), channel_id=1, replica_groups=mesh['dp'=8,'mp'=4] {'dp','mp'}, use_global_device_ids=true, to_apply=%region_51.52 | all-reduce | flops 12288 | bytes 98304 | tf_op jit(solution)/shard_map/psum | solution.py:328
  1962.4 81.9 %all-reduce.4.cloned.1.call-done = f32[50,2048]{1,0:T(8,128)} async-done(((f32[50,2048]{1,0:T(8,128)}), f32[50,2048]{1,0:T(8,128)}) %all-reduce.4.cloned.1.call-update) | async-done | bytes 409616 | tf_op jit(solution)/shard_map/psum | solution.py:328
  (579 shorter events, 627.8 us)
Async XLA Ops:
  7.2 33.2 %all-gather.21.cloned.1.call-start = ((), (), s32[]{:S(2)}) async-start(), calls=%async_computation.16 | async-start | bytes 2359296 | tf_op jit(solution)/shard_map/all_gather | solution.py:141
  7.9 114.9 %all-gather.17.cloned.1.call-start = ((), (), s32[]{:S(2)}) async-start(), calls=%async_computation.14 | async-start | bytes 5242880 | tf_op jit(solution)/shard_map/all_gather | solution.py:151
  14.1 137.6 %all-gather.19.cloned.1.call-start = ((), (), s32[]{:S(2)}) async-start(), calls=%async_computation.15 | async-start | bytes 2359296 | tf_op jit(solution)/shard_map/all_gather | solution.py:140
  14.8 166.5 %all-gather.23.cloned.1.call-start = ((), (), s32[]{:S(2)}) async-start(), calls=%async_computation.17 | async-start | bytes 2359296 | tf_op jit(solution)/shard_map/all_gather | solution.py:142
  15.4 206.4 %all-gather.25.cloned.1.call-start = ((), (), s32[]{:S(2)}) async-start(), calls=%async_computation.18 | async-start | bytes 2359296 | tf_op jit(solution)/shard_map/all_gather | solution.py:143
  16.0 277.8 %all-gather.33.cloned.1.call-start = ((), (), s32[]{:S(2)}) async-start(), calls=%async_computation.24 | async-start | bytes 5242880 | tf_op jit(solution)/shard_map/all_gather | solution.py:151
  16.6 355.3 %reduce-scatter.15.cloned.1.call-start = ((), (), s32[]{:S(2)}) async-start(), calls=%async_computation.19 | async-start | bytes 5242880 | tf_op jit(solution)/shard_map/reduce_scatter | solution.py:184
  229.0 222.6 %reduce-scatter.19.cloned.1.call-start = ((), (), s32[]{:S(2)}) async-start(), calls=%async_computation.25 | async-start | bytes 5242880 | tf_op jit(solution)/shard_map/reduce_scatter | solution.py:184
  348.3 160.6 %all-gather.29.cloned.1.call-start = ((), (), s32[]{:S(2)}) async-start(), calls=%async_computation.21 | async-start | bytes 9437184 | tf_op jit(solution)/shard_map/all_gather | solution.py:144
  349.0 242.2 %all-gather.27.cloned.1.call-start = ((), (), s32[]{:S(2)}) async-start(), calls=%async_computation.20 | async-start | bytes 5242880 | tf_op jit(solution)/shard_map/all_gather | solution.py:193
  457.4 215.3 %all-gather.41.cloned.1.call-start = ((), (), s32[]{:S(2)}) async-start(), calls=%async_computation.41 | async-start | bytes 5242880 | tf_op jit(solution)/shard_map/all_gather | solution.py:213
  459.7 269.6 %all-gather.31.cloned.1.call-start = ((), (), s32[]{:S(2)}) async-start(), calls=%async_computation.22 | async-start | bytes 9437184 | tf_op jit(solution)/shard_map/all_gather | solution.py:145
  460.3 351.0 %all-gather.35.cloned.1.call-start = ((), (), s32[]{:S(2)}) async-start(), calls=%async_computation.26 | async-start | bytes 5242880 | tf_op jit(solution)/shard_map/all_gather | solution.py:193
  461.0 431.0 %all-gather.43.cloned.1.call-start = ((), (), s32[]{:S(2)}) async-start(), calls=%async_computation.42 | async-start | bytes 5242880 | tf_op jit(solution)/shard_map/all_gather | solution.py:213
  461.6 508.5 %reduce-scatter.23.cloned.1.call-start = ((), (), s32[]{:S(2)}) async-start(), calls=%async_computation.28 | async-start | bytes 5242880 | tf_op jit(solution)/shard_map/reduce_scatter | solution.py:223
  763.2 286.4 %reduce-scatter.27.cloned.1.call-start = ((), (), s32[]{:S(2)}) async-start(), calls=%async_computation.31 | async-start | bytes 5242880 | tf_op jit(solution)/shard_map/reduce_scatter | solution.py:223
  926.2 202.9 %reduce-scatter.21.cloned.1.call-start = ((), (), s32[]{:S(2)}) async-start(), calls=%async_computation.27 | async-start | bytes 5242880 | tf_op jit(solution)/shard_map/reduce_scatter | solution.py:205
  942.4 266.2 %reduce-scatter.17.cloned.1.call-start = ((), (), s32[]{:S(2)}) async-start(), calls=%async_computation.23 | async-start | bytes 5242880 | tf_op jit(solution)/shard_map/reduce_scatter | solution.py:205
  958.7 340.3 %all-gather.39.cloned.1.call-start = ((), (), s32[]{:S(2)}) async-start(), calls=%async_computation.32 | async-start | bytes 5242880 | tf_op jit(solution)/shard_map/all_gather | solution.py:227
  1217.6 213.4 %all-gather.37.cloned.1.call-start = ((), (), s32[]{:S(2)}) async-start(), calls=%async_computation.29 | async-start | bytes 5242880 | tf_op jit(solution)/shard_map/all_gather | solution.py:227
  1218.8 413.9 %reduce-scatter.39.cloned.1.call-start = ((), (), s32[]{:S(2)}) async-start(), calls=%async_computation.39 | async-start | bytes 9437184 | tf_op jit(solution)/shard_map/reduce_scatter | solution.py:320
  1249.1 386.4 %reduce-scatter.41.cloned.1.call-start = ((), (), s32[]{:S(2)}) async-start(), calls=%async_computation.40 | async-start | bytes 9437184 | tf_op jit(solution)/shard_map/reduce_scatter | solution.py:323
  1288.4 375.1 %reduce-scatter.31.cloned.1.call-start = ((), (), s32[]{:S(2)}) async-start(), calls=%async_computation.35 | async-start | bytes 2359296 | tf_op jit(solution)/shard_map/reduce_scatter | solution.py:308
  1572.0 93.3 %reduce-scatter.33.cloned.1.call-start = ((), (), s32[]{:S(2)}) async-start(), calls=%async_computation.36 | async-start | bytes 2359296 | tf_op jit(solution)/shard_map/reduce_scatter | solution.py:311
  1582.5 119.9 %reduce-scatter.35.cloned.1.call-start = ((), (), s32[]{:S(2)}) async-start(), calls=%async_computation.37 | async-start | bytes 2359296 | tf_op jit(solution)/shard_map/reduce_scatter | solution.py:314
  1593.3 153.9 %reduce-scatter.37.cloned.1.call-start = ((), (), s32[]{:S(2)}) async-start(), calls=%async_computation.38 | async-start | bytes 2359296 | tf_op jit(solution)/shard_map/reduce_scatter | solution.py:317
  1601.9 224.3 %reduce-scatter.25.cloned.1.call-start = ((), (), s32[]{:S(2)}) async-start(), calls=%async_computation.30 | async-start | bytes 5242880 | tf_op jit(solution)/shard_map/reduce_scatter | solution.py:279
  1614.4 292.1 %reduce-scatter.29.cloned.1.call-start = ((), (), s32[]{:S(2)}) async-start(), calls=%async_computation.33 | async-start | bytes 5242880 | tf_op jit(solution)/shard_map/reduce_scatter | solution.py:279
  1627.5 416.8 %all-reduce.4.cloned.1.call-start = ((), (), s32[]{:S(2)}) async-start(), calls=%async_computation.34 | async-start | bytes 917504 | tf_op jit(solution)/shard_map/psum | solution.py:328
  1635.5 190.7 %copy-start.77 = (f32[256]{0:T(256)S(1)}, f32[256]{0:T(256)}, u32[]{:S(2)}) copy-start(f32[256]{0:T(256)} %copy-done.76) | copy-start | bytes 3076
  1638.5 268.0 %copy-start.71 = (f32[256]{0:T(256)S(1)}, f32[256]{0:T(256)}, u32[]{:S(2)}) copy-start(f32[256]{0:T(256)} %copy-done.70) | copy-start | bytes 3076
  1638.5 268.0 %copy-start.79 = (f32[256]{0:T(256)S(1)}, f32[256]{0:T(256)}, u32[]{:S(2)}) copy-start(f32[256]{0:T(256)} %copy-done.78) | copy-start | bytes 3076
  (149 other events, 2654.6 us)
Sparse Core Ops, SparseCore 0:
  9.9 30.3 all-gather.20
  42.5 80.3 all-gather.16
  124.8 26.8 all-gather.18
  153.4 27.8 all-gather.22
  183.1 28.1 all-gather.24
  213.3 80.4 all-gather.32
  296.6 75.2 reduce-scatter.14
  374.3 77.2 reduce-scatter.18
  453.5 55.2 all-gather.28
  510.8 80.3 all-gather.26
  593.3 79.2 all-gather.40
  674.4 54.8 all-gather.30
  730.9 80.3 all-gather.34
  812.7 79.2 all-gather.42
  894.8 75.3 reduce-scatter.22
  972.4 77.2 reduce-scatter.26
  1051.8 77.2 reduce-scatter.20
  1131.3 77.2 reduce-scatter.16
  1217.7 81.2 all-gather.38
  1300.4 79.2 all-gather.36
  1383.2 69.7 reduce-scatter.38
  1456.9 71.2 reduce-scatter.40
  1572.2 40.9 reduce-scatter.30
  1616.6 41.3 reduce-scatter.32
  1661.3 41.1 reduce-scatter.34
  1706.0 41.2 reduce-scatter.36
  1749.4 76.7 reduce-scatter.24
  1829.2 77.2 reduce-scatter.28
  1916.7 127.5 all-reduce.3
where the time goes:
time: 2060 us; the launch traced here: 2050 us
  waiting for transfers between devices  1260 us (61%)
  matrix products  513 us (25%)
  other arithmetic  122 us (6%)
  blocking collectives  64 us (3%)
  local copies, waits for them, and re-layouts  56.1 us (3%)
    reduce_scatter x2, waiting for transfers between devices, shards(): lax.psum_scatter((times_t(grad_query, query_full) * qk_scale + times_t(gr...  155 us
    reduce_scatter x2, waiting for transfers between devices, shards(): lax.psum_scatter(dense(active, down_full).astype(jnp.bfloat16), 'mp', sca...  155 us
    all_gather x2, waiting for transfers between devices, shards(): lax.all_gather(normed.astype(jnp.bfloat16), 'mp', axis=0, tiled=True)  147 us
    all_gather x2, waiting for transfers between devices, shards(): mlp_shard_rows = lax.all_gather(grad_rows, 'mp', axis=0, tiled=True)  133 us
    all_gather x2, waiting for transfers between devices, shards(): lax.all_gather(normed_two.astype(jnp.bfloat16), 'mp', axis=0, tiled=True)  130 us
    dot_general x12, matrix products, dense(): return jnp.dot(left_side, right_side, preferred_element_type=jnp.float32)  105 us
    reduce_scatter x2, waiting for transfers between devices, shards(): lax.psum_scatter(dense(attended, out_full).astype(jnp.bfloat16), 'mp', sc...  103 us
    dot_general x12, matrix products, times_t(): lax.dot_general(left_side, right_side, (((1,), (1,)), ((), ())), preferre...  101 us
  transfers between devices with their start and end apart: 29, of which 23 were waited for; matrix products, arithmetic and copies ran while one was open for 31% of the time, Pallas kernels for 0%

commit v1 on v0

--- a/solution.py
+++ b/solution.py
@@ -1,3 +1,4 @@
+import functools
 import math
 import jax
 import jax.numpy as jnp
@@ -9,6 +10,24 @@
 SUMM = 50
 precise = lax.Precision.HIGHEST
 gelu_coef = math.sqrt(2.0 / math.pi)
+
+
+def search_table(a0, axis_name):
+    fan = lax.axis_size(axis_name)
+    newest = [(dd - 1, dd) for dd in range(1, fan)] + [(fan - 1, 0)]
+    reply = a0
+    crops = [reply]
+    kk = 0
+    while kk < fan - 1:
+        reply = lax.ppermute(reply, axis_name, newest)
+        crops += [reply]
+        kk += 1
+    piece_out = jnp.concatenate([*reversed(crops)], 0)
+    latest = lax.axis_index(axis_name)
+    return jnp.roll(piece_out, (latest + 1) * reply.shape[0], 0)
+
+
+bring_the_marks = functools.partial(search_table, axis_name="mp")
 
 
 def gelu_slope(values_in):
@@ -210,7 +229,7 @@
         outputs.append(layer_rows.astype(jnp.bfloat16))
         grad_rows = cotangent[micro_step]
         grad_layer = grad_rows.astype(jnp.float32)
-        mlp_shard_rows = lax.all_gather(grad_rows, "mp", axis=0, tiled=True)
+        mlp_shard_rows = bring_the_marks(grad_rows)
         mlp_up_value = dense(normed_two_full, up_full) + bias_up
         grad_active = times_t(mlp_shard_rows, down_full)
         mlp_grad_up = (grad_active * gelu_slope(mlp_up_value)).astype(jnp.bfloat16)

time: 2060 us -> 1950 us (0.947)
  waiting for transfers between devices: 1260 us -> 1150 us
  matrix products: 513 us -> 466 us
  other arithmetic: 122 us -> 157 us
  starting transfers between devices: 2.06 us -> 29.2 us
    ppermute x0 -> x6, waiting for transfers between devices: none -> 139 us  [search_table(): reply = lax.ppermute(reply, axis_name, newest)]
    all_gather x2 -> x0, waiting for transfers between devices: 133 us -> none  [shards(): mlp_shard_rows = lax.all_gather(grad_rows, 'mp', axis=0, tiled=True)]
    all_gather x2, waiting for transfers between devices: 130 us -> 52 us  [shards(): lax.all_gather(normed_two.astype(jnp.bfloat16), 'mp', axis=0, tiled=True)]
    all_gather x2, waiting for transfers between devices: 10.6 us -> 80.2 us  [shards(): lax.all_gather(grad_mixed.astype(jnp.bfloat16), 'mp', axis=0, tiled=True)]
    all_gather x1, waiting for transfers between devices: 47.2 us -> 0.02 us  [shards(): lax.all_gather(up_weight, 'dp', axis=0, tiled=True)]
    reduce_scatter x1, waiting for transfers between devices: 42.9 us -> 0.01 us  [shards(): lax.psum_scatter(full_sums[3].astype(jnp.bfloat16), 'dp', scatter_dimensi...]
    reduce_scatter x1, waiting for transfers between devices: 0.01 us -> 41.3 us  [shards(): lax.psum_scatter(full_sums[1].astype(jnp.bfloat16), 'dp', scatter_dimensi...]
    reduce_scatter x1, waiting for transfers between devices: 35.3 us -> 0.01 us  [shards(): lax.psum_scatter(full_sums[2].astype(jnp.bfloat16), 'dp', scatter_dimensi...]
  transfers between devices with their start and end apart: 29 -> 33, of which waited for: 23 -> 24; matrix products, arithmetic and copies ran while one was open for 31% -> 32% of each run, Pallas kernels for 0% -> 0%
where the time goes in v1:
time: 1950 us; the launch traced here: 1940 us
  waiting for transfers between devices  1150 us (59%)
  matrix products  466 us (24%)
  other arithmetic  157 us (8%)
  blocking collectives  64.1 us (3%)
  local copies, waits for them, and re-layouts  39.8 us (2%)
  starting transfers between devices  29.2 us (1%)
    reduce_scatter x2, waiting for transfers between devices, shards(): lax.psum_scatter((times_t(grad_query, query_full) * qk_scale + times_t(gr...  155 us
    reduce_scatter x2, waiting for transfers between devices, shards(): lax.psum_scatter(dense(active, down_full).astype(jnp.bfloat16), 'mp', sca...  155 us
    all_gather x2, waiting for transfers between devices, shards(): lax.all_gather(normed.astype(jnp.bfloat16), 'mp', axis=0, tiled=True)  148 us
    ppermute x6, waiting for transfers between devices, search_table(): reply = lax.ppermute(reply, axis_name, newest)  139 us
    dot_general x12, matrix products, dense(): return jnp.dot(left_side, right_side, preferred_element_type=jnp.float32)  105 us
    reduce_scatter x2, waiting for transfers between devices, shards(): lax.psum_scatter(dense(attended, out_full).astype(jnp.bfloat16), 'mp', sc...  104 us
    dot_general x12, matrix products, inner_rows(): lax.dot_general(left_side, right_side, (((0,), (0,)), ((), ())), preferre...  103 us
    dot_general x12, matrix products, times_t(): lax.dot_general(left_side, right_side, (((1,), (1,)), ((), ())), preferre...  95.2 us
  transfers between devices with their start and end apart: 33, of which 24 were waited for; matrix products, arithmetic and copies ran while one was open for 32% of the time, Pallas kernels for 0%

profile of v1, /device:TPU:1, one launch (start us, length us, event | category | flops | bytes accessed | tf_op | source)
XLA Modules:
  0.0 1937.9 jit_solution(14688139732212548663)
XLA Ops:
  17.3 23.1 %all-gather.17.cloned.1.call-done = bf16[2048,512]{1,0:T(8,128)(2,1)} async-done(((bf16[256,512]{1,0:T(8,128)(2,1)}), bf16[2048,512]{1,0:T(8,128)(2,1)}) %all-gather.17.cloned.1.call-update) | async-done | bytes 2097168 | tf_op jit(solution)/shard_map/all_gather | solution.py:160
  40.4 82.5 %all-gather.13.cloned.1.call-done = bf16[1024,2048]{1,0:T(8,128)(2,1)} async-done(((bf16[256,2048]{1,0:T(8,128)(2,1)}), bf16[1024,2048]{1,0:T(8,128)(2,1)}) %all-gather.13.cloned.1.call-update) | async-done | bytes 4194320 | tf_op jit(solution)/shard_map/all_gather | solution.py:170
  128.1 23.5 %all-gather.19.cloned.1.call-done = bf16[2048,512]{1,0:T(8,128)(2,1)} async-done(((bf16[256,512]{1,0:T(8,128)(2,1)}), bf16[2048,512]{1,0:T(8,128)(2,1)}) %all-gather.19.cloned.1.call-update) | async-done | bytes 2097168 | tf_op jit(solution)/shard_map/all_gather | solution.py:161
  157.9 23.4 %all-gather.15.cloned.1.call-done = bf16[2048,512]{1,0:T(8,128)(2,1)} async-done(((bf16[256,512]{1,0:T(8,128)(2,1)}), bf16[2048,512]{1,0:T(8,128)(2,1)}) %all-gather.15.cloned.1.call-update) | async-done | bytes 2097168 | tf_op jit(solution)/shard_map/all_gather | solution.py:159
  187.6 33.4 %while.56 = (s32[]{:T(128)}, bf16[2,512,512]{2,1,0:T(8,128)(2,1)}, f32[2,8,512]{2,1,0:T(8,128)S(1)}, s32[2]{0:T(128)S(1)}, bf16[1024,8,64]{0,2,1:T(8,128)(2,1)S(...) while((s32[]{:T(128)}, bf16[2,512,512]{2,1,0:T(8,128)(2,1)}, ...), condition=%wide.region_5.6_spmd.clone, body=%wide.region_2.5_spmd.clone.sunk | while | flops 1112807936 | bytes 62003432 | solution.py:199
  228.6 65.1 %all-gather.29.cloned.1.call-done = bf16[1024,2048]{1,0:T(8,128)(2,1)} async-done(((bf16[256,2048]{1,0:T(8,128)(2,1)}), bf16[1024,2048]{1,0:T(8,128)(2,1)}) %all-gather.29.cloned.1.call-update) | async-done | bytes 4194320 | tf_op jit(solution)/shard_map/all_gather | solution.py:170
  307.1 33.0 %while.57 = (s32[]{:T(128)}, bf16[2,512,512]{2,1,0:T(8,128)(2,1)}, f32[2,8,512]{2,1,0:T(8,128)S(1)}, s32[2]{0:T(128)S(1)}, bf16[1024,8,64]{0,2,1:T(8,128)(2,1)S(...) while((s32[]{:T(128)}, bf16[2,512,512]{2,1,0:T(8,128)(2,1)}, ...), condition=%wide.region_15.16_spmd.clone, body=%wide.region_12.15_spmd.clone.sunk | while | flops 1112807936 | bytes 62003432 | solution.py:199
  348.1 23.8 %reduce-scatter.15.cloned.1.call-done = bf16[256,2048]{1,0:T(8,128)(2,1)} async-done(((bf16[1024,2048]{1,0:T(8,128)(2,1)}), bf16[256,2048]{1,0:T(8,128)(2,1)}) %reduce-scatter.15.cloned.1.call-update) | async-done | bytes 1048592 | tf_op jit(solution)/shard_map/reduce_scatter | solution.py:203
  371.9 79.7 %reduce-scatter.19.cloned.1.call-done = bf16[256,2048]{1,0:T(8,128)(2,1)} async-done(((bf16[1024,2048]{1,0:T(8,128)(2,1)}), bf16[256,2048]{1,0:T(8,128)(2,1)}) %reduce-scatter.19.cloned.1.call-update) | async-done | bytes 1048592 | tf_op jit(solution)/shard_map/reduce_scatter | solution.py:203
  461.4 22.9 %collective-permute-done.3 = bf16[256,2048]{1,0:T(8,128)(2,1)S(1)} collective-permute-done((bf16[256,2048]{1,0:T(8,128)(2,1)S(1)}, bf16[256,2048]{1,0:T(8,128)(2,1)S(1)}, u32[]{:S(2)}, u32[]{:S(2)}) %collective-permute-start.3) | collective-permute-done | bytes 1048608 | tf_op jit(solution)/shard_map/ppermute | solution.py:22
  484.3 22.5 %collective-permute-done = bf16[256,2048]{1,0:T(8,128)(2,1)S(1)} collective-permute-done((bf16[256,2048]{1,0:T(8,128)(2,1)S(1)}, bf16[256,2048]{1,0:T(8,128)(2,1)S(1)}, u32[]{:S(2)}, u32[]{:S(2)}) %collective-permute-start) | collective-permute-done | bytes 1048608 | tf_op jit(solution)/shard_map/ppermute | solution.py:22
  506.7 28.2 %collective-permute-done.4 = bf16[256,2048]{1,0:T(8,128)(2,1)} collective-permute-done((bf16[256,2048]{1,0:T(8,128)(2,1)S(1)}, bf16[256,2048]{1,0:T(8,128)(2,1)}, u32[]{:S(2)}, u32[]{:S(2)}) %collective-permute-start.4) | collective-permute-done | bytes 1048608 | tf_op jit(solution)/shard_map/ppermute | solution.py:22
  540.7 39.2 %collective-permute-done.1 = bf16[256,2048]{1,0:T(8,128)(2,1)} collective-permute-done((bf16[256,2048]{1,0:T(8,128)(2,1)S(1)}, bf16[256,2048]{1,0:T(8,128)(2,1)}, u32[]{:S(2)}, u32[]{:S(2)}) %collective-permute-start.1) | collective-permute-done | bytes 1048608 | tf_op jit(solution)/shard_map/ppermute | solution.py:22
  579.9 18.5 collective-permute-start.2
  598.4 26.4 %collective-permute-done.5 = bf16[256,2048]{1,0:T(8,128)(2,1)} collective-permute-done((bf16[256,2048]{1,0:T(8,128)(2,1)}, bf16[256,2048]{1,0:T(8,128)(2,1)}, u32[]{:S(2)}, u32[]{:S(2)}) %collective-permute-start.5) | collective-permute-done | bytes 1048608 | tf_op jit(solution)/shard_map/ppermute | solution.py:22
  639.9 18.8 all-gather.31.cloned.1.call-done
  673.5 41.6 %all-gather.27.cloned.1.call-done = bf16[2048,2048]{1,0:T(8,128)(2,1)} async-done(((bf16[2048,256]{1,0:T(8,128)(2,1)}), bf16[2048,2048]{1,0:T(8,128)(2,1)}) %all-gather.27.cloned.1.call-update) | async-done | bytes 8388624 | tf_op jit(solution)/shard_map/all_gather | solution.py:164
  715.1 18.9 convert_reduce_fusion
  764.3 33.2 %all-gather.23.cloned.1.call-done = bf16[1024,2048]{1,0:T(8,128)(2,1)} async-done(((bf16[256,2048]{1,0:T(8,128)(2,1)}), bf16[1024,2048]{1,0:T(8,128)(2,1)}) %all-gather.23.cloned.1.call-update) | async-done | bytes 4194320 | tf_op jit(solution)/shard_map/all_gather | solution.py:212
  876.0 78.7 %reduce-scatter.23.cloned.1.call-done = bf16[256,2048]{1,0:T(8,128)(2,1)} async-done(((bf16[1024,2048]{1,0:T(8,128)(2,1)}), bf16[256,2048]{1,0:T(8,128)(2,1)}) %reduce-scatter.23.cloned.1.call-update) | async-done | bytes 1048592 | tf_op jit(solution)/shard_map/reduce_scatter | solution.py:242
  958.7 75.4 %reduce-scatter.21.cloned.1.call-done = bf16[256,2048]{1,0:T(8,128)(2,1)} async-done(((bf16[1024,2048]{1,0:T(8,128)(2,1)}), bf16[256,2048]{1,0:T(8,128)(2,1)}) %reduce-scatter.21.cloned.1.call-update) | async-done | bytes 1048592 | tf_op jit(solution)/shard_map/reduce_scatter | solution.py:224
  1034.1 79.5 %reduce-scatter.17.cloned.1.call-done = bf16[256,2048]{1,0:T(8,128)(2,1)} async-done(((bf16[1024,2048]{1,0:T(8,128)(2,1)}), bf16[256,2048]{1,0:T(8,128)(2,1)}) %reduce-scatter.17.cloned.1.call-update) | async-done | bytes 1048592 | tf_op jit(solution)/shard_map/reduce_scatter | solution.py:224
  1141.6 21.4 %add_convert_fusion = bf16[2048,2048]{1,0:T(8,128)(2,1)} fusion(f32[2048,2048]{1,0:T(8,128)} %fusion.173, bf16[1024,2048]{1,0:T(8,128)(2,1)S(1)} %copy-done.43, f32[1024,2048]{1,0:T(8,128)} %fusion.185, f32[2048]{0:T(1024)S(1)} %convert_element_type.266), kind=kOutput, calls=%fused_computation.128 | convolution fusion | flops 8619294720 | bytes 37756928 | tf_op jit(solution)/shard_map/dot_general | solution.py:69
  1215.0 69.9 %all-gather.35.cloned.1.call-done = bf16[1024,2048]{1,0:T(8,128)(2,1)} async-done(((bf16[256,2048]{1,0:T(8,128)(2,1)}), bf16[1024,2048]{1,0:T(8,128)(2,1)}) %all-gather.35.cloned.1.call-update) | async-done | bytes 4194320 | tf_op jit(solution)/shard_map/all_gather | solution.py:246
  1293.1 96.2 %while.58 = (s32[]{:T(128)}, f32[1024,8,64]{0,2,1:T(8,128)}, f32[1024,8,64]{0,2,1:T(8,128)}, bf16[2,512,512]{1,2,0:T(8,128)(2,1)}, s32[2]{0:T(128)S(1)}, /*index...) while((s32[]{:T(128)}, f32[1024,8,64]{0,2,1:T(8,128)}, ...), condition=%wide.region_25.27_spmd.clone, body=%wide.region_23.26_spmd.clone.sunk | while | flops 2738100736 | bytes 193583536 | solution.py:287
  1396.9 94.4 %while.59 = (s32[]{:T(128)}, f32[1024,8,64]{0,2,1:T(8,128)}, f32[1024,8,64]{0,2,1:T(8,128)}, bf16[2,512,512]{1,2,0:T(8,128)(2,1)}, s32[2]{0:T(128)S(1)}, /*index...) while((s32[]{:T(128)}, f32[1024,8,64]{0,2,1:T(8,128)}, ...), condition=%wide.region_34.36_spmd.clone, body=%wide.region_32.35_spmd.clone.sunk | while | flops 2738100736 | bytes 193583536 | solution.py:287
  1562.7 22.3 %all-reduce.1 = (f32[512]{0:T(512)}, f32[512]{0:T(512)}, f32[2048]{0:T(1024)}) all-reduce(f32[512]{0:T(512)S(1)} %add_multiply_fusion, f32[512]{0:T(512)S(1)} %add.519, f32[2048]{0:T(1024)S(1)} %add.523), channel_id=1, replica_groups=mesh['dp'=8,'mp'=4] {'dp'}, use_global_device_ids=true, to_apply=%region_42.44 | all-reduce | flops 3072 | bytes 24576 | tf_op jit(solution)/shard_map/psum | solution.py:346
  1590.4 41.3 %reduce-scatter.33.cloned.1.call-done = bf16[256,512]{1,0:T(8,128)(2,1)} async-done(((bf16[2048,512]{1,0:T(8,128)(2,1)}), bf16[256,512]{1,0:T(8,128)(2,1)}) %reduce-scatter.33.cloned.1.call-update) | async-done | bytes 262160 | tf_op jit(solution)/shard_map/reduce_scatter | solution.py:330
  1633.5 77.3 %reduce-scatter.25.cloned.1.call-done = bf16[256,2048]{1,0:T(8,128)(2,1)} async-done(((bf16[1024,2048]{1,0:T(8,128)(2,1)}), bf16[256,2048]{1,0:T(8,128)(2,1)}) %reduce-scatter.25.cloned.1.call-update) | async-done | bytes 1048592 | tf_op jit(solution)/shard_map/reduce_scatter | solution.py:298
  1713.1 77.9 %reduce-scatter.29.cloned.1.call-done = bf16[256,2048]{1,0:T(8,128)(2,1)} async-done(((bf16[1024,2048]{1,0:T(8,128)(2,1)}), bf16[256,2048]{1,0:T(8,128)(2,1)}) %reduce-scatter.29.cloned.1.call-update) | async-done | bytes 1048592 | tf_op jit(solution)/shard_map/reduce_scatter | solution.py:298
  1801.1 41.8 %all-reduce = (f32[2048]{0:T(1024)}, f32[2048]{0:T(1024)}, f32[2048]{0:T(1024)}, f32[2048]{0:T(1024)}, f32[2048]{0:T(1024)}, /*index=5*/f32[2048]{0:T(1024)}) all-reduce(f32[2048]{0:T(1024)S(1)} %add.521, f32[2048]{0:T(1024)S(1)} %add.525, f32[2048]{0:T(1024)S(1)} %add.526, ...), channel_id=1, replica_groups=mesh['dp'=8,'mp'=4] {'dp','mp'}, use_global_device_ids=true, to_apply=%region_51.53 | all-reduce | flops 12288 | bytes 98304 | tf_op jit(solution)/shard_map/psum | solution.py:347
  1846.9 81.9 %all-reduce.4.cloned.1.call-done = f32[50,2048]{1,0:T(8,128)} async-done(((f32[50,2048]{1,0:T(8,128)}), f32[50,2048]{1,0:T(8,128)}) %all-reduce.4.cloned.1.call-update) | async-done | bytes 409616 | tf_op jit(solution)/shard_map/psum | solution.py:347
  (536 shorter events, 647.8 us)
Async XLA Ops:
  7.2 33.2 %all-gather.17.cloned.1.call-start = ((), (), s32[]{:S(2)}) async-start(), calls=%async_computation.16 | async-start | bytes 2359296 | tf_op jit(solution)/shard_map/all_gather | solution.py:160
  7.9 114.9 %all-gather.13.cloned.1.call-start = ((), (), s32[]{:S(2)}) async-start(), calls=%async_computation.14 | async-start | bytes 5242880 | tf_op jit(solution)/shard_map/all_gather | solution.py:170
  14.1 137.6 %all-gather.19.cloned.1.call-start = ((), (), s32[]{:S(2)}) async-start(), calls=%async_computation.17 | async-start | bytes 2359296 | tf_op jit(solution)/shard_map/all_gather | solution.py:161
  14.8 166.5 %all-gather.15.cloned.1.call-start = ((), (), s32[]{:S(2)}) async-start(), calls=%async_computation.15 | async-start | bytes 2359296 | tf_op jit(solution)/shard_map/all_gather | solution.py:159
  15.4 205.6 %all-gather.21.cloned.1.call-start = ((), (), s32[]{:S(2)}) async-start(), calls=%async_computation.18 | async-start | bytes 2359296 | tf_op jit(solution)/shard_map/all_gather | solution.py:162
  16.0 277.7 %all-gather.29.cloned.1.call-start = ((), (), s32[]{:S(2)}) async-start(), calls=%async_computation.24 | async-start | bytes 5242880 | tf_op jit(solution)/shard_map/all_gather | solution.py:170
  16.6 355.3 %reduce-scatter.15.cloned.1.call-start = ((), (), s32[]{:S(2)}) async-start(), calls=%async_computation.19 | async-start | bytes 5242880 | tf_op jit(solution)/shard_map/reduce_scatter | solution.py:203
  228.4 223.2 %reduce-scatter.19.cloned.1.call-start = ((), (), s32[]{:S(2)}) async-start(), calls=%async_computation.25 | async-start | bytes 5242880 | tf_op jit(solution)/shard_map/reduce_scatter | solution.py:203
  347.3 292.6 %all-gather.25.cloned.1.call-start = ((), (), s32[]{:S(2)}) async-start(), calls=%async_computation.21 | async-start | bytes 9437184 | tf_op jit(solution)/shard_map/all_gather | solution.py:163
  348.0 310.7 %all-gather.31.cloned.1.call-start = ((), (), s32[]{:S(2)}) async-start(), calls=%async_computation.26 | async-start | bytes 5242880 | tf_op jit(solution)/shard_map/all_gather | solution.py:212
  457.4 257.7 %all-gather.27.cloned.1.call-start = ((), (), s32[]{:S(2)}) async-start(), calls=%async_computation.22 | async-start | bytes 9437184 | tf_op jit(solution)/shard_map/all_gather | solution.py:164
  458.2 339.3 %all-gather.23.cloned.1.call-start = ((), (), s32[]{:S(2)}) async-start(), calls=%async_computation.20 | async-start | bytes 5242880 | tf_op jit(solution)/shard_map/all_gather | solution.py:212
  459.7 47.1 %collective-permute-start = (bf16[256,2048]{1,0:T(8,128)(2,1)S(1)}, bf16[256,2048]{1,0:T(8,128)(2,1)S(1)}, u32[]{:S(2)}, u32[]{:S(2)}) collective-permute-start(bf16[256,2048]{1,0:T(8,128)(2,1)S(1)} %get-tuple-element.482), channel_id=1, source_target_pairs={{0,1},{1,2},{2,3},{3,0},{4,5},{5,6},{6,7},{7,4},{8,9},{9,10},{10,1... | collective-permute-start | bytes 3145736 | tf_op jit(solution)/shard_map/ppermute | solution.py:22
  484.3 50.7 %collective-permute-start.4 = (bf16[256,2048]{1,0:T(8,128)(2,1)S(1)}, bf16[256,2048]{1,0:T(8,128)(2,1)}, u32[]{:S(2)}, u32[]{:S(2)}) collective-permute-start(bf16[256,2048]{1,0:T(8,128)(2,1)S(1)} %collective-permute-done.3), channel_id=1, source_target_pairs={{0,1},{1,2},{2,3},{3,0},{4,5},{5,6},{6,7},{7,4},{8,9},{9,10},{10,1... | collective-permute-start | bytes 3145736 | tf_op jit(solution)/shard_map/ppermute | solution.py:22
  506.7 73.2 %collective-permute-start.1 = (bf16[256,2048]{1,0:T(8,128)(2,1)S(1)}, bf16[256,2048]{1,0:T(8,128)(2,1)}, u32[]{:S(2)}, u32[]{:S(2)}) collective-permute-start(bf16[256,2048]{1,0:T(8,128)(2,1)S(1)} %collective-permute-done), channel_id=1, source_target_pairs={{0,1},{1,2},{2,3},{3,0},{4,5},{5,6},{6,7},{7,4},{8,9},{9,10},{10,1... | collective-permute-start | bytes 3145736 | tf_op jit(solution)/shard_map/ppermute | solution.py:22
  535.0 89.9 %collective-permute-start.5 = (bf16[256,2048]{1,0:T(8,128)(2,1)}, bf16[256,2048]{1,0:T(8,128)(2,1)}, u32[]{:S(2)}, u32[]{:S(2)}) collective-permute-start(bf16[256,2048]{1,0:T(8,128)(2,1)} %collective-permute-done.4), channel_id=1, source_target_pairs={{0,1},{1,2},{2,3},{3,0},{4,5},{5,6},{6,7},{7,4},{8,9},{9,10},{10,1... | collective-permute-start | bytes 3145736 | tf_op jit(solution)/shard_map/ppermute | solution.py:22
  579.9 166.6 %collective-permute-start.2 = (bf16[256,2048]{1,0:T(8,128)(2,1)}, bf16[256,2048]{1,0:T(8,128)(2,1)}, u32[]{:S(2)}, u32[]{:S(2)}) collective-permute-start(bf16[256,2048]{1,0:T(8,128)(2,1)} %collective-permute-done.1), channel_id=1, source_target_pairs={{0,1},{1,2},{2,3},{3,0},{4,5},{5,6},{6,7},{7,4},{8,9},{9,10},{10,1... | collective-permute-start | bytes 3145736 | tf_op jit(solution)/shard_map/ppermute | solution.py:22
  639.8 236.1 %reduce-scatter.27.cloned.1.call-start = ((), (), s32[]{:S(2)}) async-start(), calls=%async_computation.31 | async-start | bytes 5242880 | tf_op jit(solution)/shard_map/reduce_scatter | solution.py:242
  746.4 208.3 %reduce-scatter.23.cloned.1.call-start = ((), (), s32[]{:S(2)}) async-start(), calls=%async_computation.28 | async-start | bytes 5242880 | tf_op jit(solution)/shard_map/reduce_scatter | solution.py:242
  842.8 191.3 %reduce-scatter.21.cloned.1.call-start = ((), (), s32[]{:S(2)}) async-start(), calls=%async_computation.27 | async-start | bytes 5242880 | tf_op jit(solution)/shard_map/reduce_scatter | solution.py:224
  859.2 254.5 %reduce-scatter.17.cloned.1.call-start = ((), (), s32[]{:S(2)}) async-start(), calls=%async_computation.23 | async-start | bytes 5242880 | tf_op jit(solution)/shard_map/reduce_scatter | solution.py:224
  875.4 328.8 %all-gather.33.cloned.1.call-start = ((), (), s32[]{:S(2)}) async-start(), calls=%async_computation.29 | async-start | bytes 5242880 | tf_op jit(solution)/shard_map/all_gather | solution.py:246
  1122.8 162.2 %all-gather.35.cloned.1.call-start = ((), (), s32[]{:S(2)}) async-start(), calls=%async_computation.32 | async-start | bytes 5242880 | tf_op jit(solution)/shard_map/all_gather | solution.py:246
  1124.0 429.9 %reduce-scatter.41.cloned.1.call-start = ((), (), s32[]{:S(2)}) async-start(), calls=%async_computation.40 | async-start | bytes 9437184 | tf_op jit(solution)/shard_map/reduce_scatter | solution.py:342
  1163.0 393.7 %reduce-scatter.39.cloned.1.call-start = ((), (), s32[]{:S(2)}) async-start(), calls=%async_computation.39 | async-start | bytes 9437184 | tf_op jit(solution)/shard_map/reduce_scatter | solution.py:339
  1193.9 391.2 %reduce-scatter.37.cloned.1.call-start = ((), (), s32[]{:S(2)}) async-start(), calls=%async_computation.38 | async-start | bytes 2359296 | tf_op jit(solution)/shard_map/reduce_scatter | solution.py:336
  1389.4 197.4 %reduce-scatter.35.cloned.1.call-start = ((), (), s32[]{:S(2)}) async-start(), calls=%async_computation.37 | async-start | bytes 2359296 | tf_op jit(solution)/shard_map/reduce_scatter | solution.py:333
  1501.8 86.8 %reduce-scatter.31.cloned.1.call-start = ((), (), s32[]{:S(2)}) async-start(), calls=%async_computation.35 | async-start | bytes 2359296 | tf_op jit(solution)/shard_map/reduce_scatter | solution.py:327
  1512.9 118.8 %reduce-scatter.33.cloned.1.call-start = ((), (), s32[]{:S(2)}) async-start(), calls=%async_computation.36 | async-start | bytes 2359296 | tf_op jit(solution)/shard_map/reduce_scatter | solution.py:330
  1523.6 187.3 %reduce-scatter.25.cloned.1.call-start = ((), (), s32[]{:S(2)}) async-start(), calls=%async_computation.30 | async-start | bytes 5242880 | tf_op jit(solution)/shard_map/reduce_scatter | solution.py:298
  1535.9 255.1 %reduce-scatter.29.cloned.1.call-start = ((), (), s32[]{:S(2)}) async-start(), calls=%async_computation.33 | async-start | bytes 5242880 | tf_op jit(solution)/shard_map/reduce_scatter | solution.py:298
  1548.8 380.0 %all-reduce.4.cloned.1.call-start = ((), (), s32[]{:S(2)}) async-start(), calls=%async_computation.34 | async-start | bytes 917504 | tf_op jit(solution)/shard_map/psum | solution.py:347
  (131 other events, 3137.7 us)
Sparse Core Ops, SparseCore 0:
  9.9 30.3 all-gather.16
  42.5 80.3 all-gather.12
  124.8 26.8 all-gather.18
  153.4 27.8 all-gather.14
  183.1 28.1 all-gather.20
  213.3 80.3 all-gather.28
  296.6 75.2 reduce-scatter.14
  374.3 77.2 reduce-scatter.18
  453.5 55.2 all-gather.24
  510.8 147.8 all-gather.30
  660.6 54.4 all-gather.26
  717.1 80.3 all-gather.22
  799.8 75.2 reduce-scatter.26
  877.4 77.2 reduce-scatter.22
  956.8 77.2 reduce-scatter.20
  1036.4 77.2 reduce-scatter.16
  1122.9 81.2 all-gather.32
  1205.6 79.2 all-gather.34
  1288.4 69.7 reduce-scatter.40
  1361.9 71.2 reduce-scatter.38
  1436.5 41.2 reduce-scatter.36
  1502.0 40.2 reduce-scatter.34
  1545.6 41.3 reduce-scatter.30
  1590.4 41.2 reduce-scatter.32
  1634.0 76.7 reduce-scatter.24
  1713.7 77.2 reduce-scatter.28
  1801.2 127.5 all-reduce.3
